TPU v7x, 32 devices: a whole 2x2x4 slice. The times are simulated.
32 devices in a mesh: fsdp: 8 (over z, y), rep: 4 (over x, core).
Axes of the slice: x: 2, y: 2, z: 4, core: 2. Of those that a mesh axis runs over, the one named last changes fastest.
Arguments:
- tokens: bfloat16 [64, 512, 768], P(('fsdp', 'rep')), may hold values from -6 to 6
- page_ids: int32 [64, 512], P(('fsdp', 'rep')), may hold values from 0 to 7, never falling along the last dimension, each value on 1 to 128 neighbouring positions
- box_coords: int32 [8, 64, 512], P(None, ('fsdp', 'rep')), may hold values from 0 to 1000
- w_qkv: bfloat16 [768, 2304], P('fsdp'), may hold values from -0.3125 to 0.3125
- b_qkv: bfloat16 [2304], P('fsdp'), may hold values from -3 to 3
- w_pos: bfloat16 [24576], P('fsdp'), may hold values from -0.75 to 0.75
- w_out: bfloat16 [768, 768], P('fsdp'), may hold values from -0.875 to 0.875
- b_out: bfloat16 [768], P('fsdp'), may hold values from -3 to 3
- gain_one: bfloat16 [768], P('fsdp'), may hold values from 0.5 to 1.5
- shift_one: bfloat16 [768], P('fsdp'), may hold values from -3 to 3
- w_up: bfloat16 [768, 3072], P('fsdp'), may hold values from -0.21875 to 0.21875
- b_up: bfloat16 [3072], P('fsdp'), may hold values from -3 to 3
- w_down: bfloat16 [3072, 768], P('fsdp'), may hold values from -0.109375 to 0.109375
- b_down: bfloat16 [768], P('fsdp'), may hold values from -3 to 3
- gain_two: bfloat16 [768], P('fsdp'), may hold values from 0.5 to 1.5
- shift_two: bfloat16 [768], P('fsdp'), may hold values from -3 to 3
- cotangent: bfloat16 [64, 512, 768], P(('fsdp', 'rep')), may hold values from -6 to 6
Outputs:
- layer_out: bfloat16 [64, 512, 768], P(('fsdp', 'rep'))
- grad_tokens: bfloat16 [64, 512, 768], P(('fsdp', 'rep'))
- grad_w_qkv: float32 [768, 2304], P('fsdp')
- grad_b_qkv: float32 [2304], P('fsdp')
- grad_w_pos: float32 [24576], P('fsdp')
- grad_w_out: float32 [768, 768], P('fsdp')
- grad_b_out: float32 [768], P('fsdp')
- grad_gain_one: float32 [768], P('fsdp')
- grad_shift_one: float32 [768], P('fsdp')
- grad_w_up: float32 [768, 3072], P('fsdp')
- grad_b_up: float32 [3072], P('fsdp')
- grad_w_down: float32 [3072, 768], P('fsdp')
- grad_b_down: float32 [768], P('fsdp')
- grad_gain_two: float32 [768], P('fsdp')
- grad_shift_two: float32 [768], P('fsdp')
Inputs may be any that keep to these rules, and one draw needn't show every extreme that they name: `page_ids`: within a row page ids never fall; every page holds 1 to 128 tokens, and one page of every row exactly 128.
All inputs are finite; a program needn't handle non-finite values.
Results may differ from a plain program's by a relative error of at most 0.017.
Values may be sent and summed in bfloat16 or wider, within the bound.
No kernel may reach another device: no remote copies, remote signals or barrier semaphores. Data moves between devices by JAX's collectives and lax.ppermute only.
A program may use at most 256 MiB of HBM per device.

v0:
```python
import math

import jax
import jax.numpy as jnp
from jax import lax
from jax.sharding import PartitionSpec as P

HEADS = 12
HD = 64
PE = 192


norm_eps = 1e-12


def layer_norm(values, gain, shift):
    center = jnp.mean(values, axis=-1, keepdims=True)
    offset = values - center
    spread = jnp.mean(offset * offset, axis=-1, keepdims=True)
    return offset * lax.rsqrt(spread + norm_eps) * gain + shift


def gelu_exact(values):
    return jax.nn.gelu(values, approximate=False)


def pair_swap(matrix):
    return matrix.reshape(PE // 2, 2, matrix.shape[-1])[:, ::-1].reshape(PE, matrix.shape[-1])


def row_scores(left_side, right_side, row_pages, score_scale):
    logits = jnp.einsum("hie,hje->hij", left_side, right_side, preferred_element_type=jnp.float32)
    same_page = row_pages[:, None] == row_pages[None, :]
    return jnp.where(same_page[None], logits * score_scale, -1e30)


def attend_row(left_side, right_side, value_heads, row_pages, score_scale):
    scores = row_scores(left_side, right_side, row_pages, score_scale)
    row_max = jnp.max(scores, axis=-1, keepdims=True)
    row_total = jnp.sum(jnp.exp(scores - row_max), axis=-1, keepdims=True)
    log_total = row_max + jnp.log(row_total)
    probs_low = jnp.exp(scores - log_total).astype(jnp.bfloat16)
    context = jnp.einsum("hij,hjd->hid", probs_low, value_heads, preferred_element_type=jnp.float32)
    return (context, log_total)


def attend_back(left_side, right_side, value_heads, row_pages, log_total, grad_ctx, score_scale):
    scores = row_scores(left_side, right_side, row_pages, score_scale)
    attn_probs = jnp.exp(scores - log_total)
    probs_low = attn_probs.astype(jnp.bfloat16)
    grad_probs = jnp.einsum(
        "hid,hjd->hij", grad_ctx, value_heads, preferred_element_type=jnp.float32
    )
    inner_sum = jnp.sum(grad_probs * attn_probs, axis=-1, keepdims=True)
    grad_logits = (attn_probs * (grad_probs - inner_sum) * score_scale).astype(jnp.bfloat16)
    grad_left = jnp.einsum(
        "hij,hje->hie", grad_logits, right_side, preferred_element_type=jnp.float32
    )
    grad_right = jnp.einsum(
        "hij,hie->hje", grad_logits, left_side, preferred_element_type=jnp.float32
    )
    grad_values = jnp.einsum(
        "hij,hid->hjd", probs_low, grad_ctx, preferred_element_type=jnp.float32
    )
    return (grad_left, grad_right, grad_values)


def body(
    tokens,
    page_ids,
    box_coords,
    w_qkv,
    b_qkv,
    w_pos,
    w_out,
    b_out,
    gain_one,
    shift_one,
    w_up,
    b_up,
    w_down,
    b_down,
    gain_two,
    shift_two,
    cotangent,
):
    row_count, seq_len, model_width = tokens.shape
    tok_count = row_count * seq_len
    score_scale = 1.0 / math.sqrt(HD + 2 * PE)
    shards = (
        w_qkv,
        w_out,
        w_up,
        w_down,
        b_qkv,
        w_pos,
        b_out,
        gain_one,
        shift_one,
        b_up,
        b_down,
        gain_two,
        shift_two,
    )
    gathered = (
        lax.all_gather(shards[0], "fsdp", axis=0, tiled=True),
        lax.all_gather(shards[1], "fsdp", axis=0, tiled=True),
        lax.all_gather(shards[2], "fsdp", axis=0, tiled=True),
        lax.all_gather(shards[3], "fsdp", axis=0, tiled=True),
        lax.all_gather(shards[4], "fsdp", axis=0, tiled=True),
        lax.all_gather(shards[5], "fsdp", axis=0, tiled=True),
        lax.all_gather(shards[6], "fsdp", axis=0, tiled=True),
        lax.all_gather(shards[7], "fsdp", axis=0, tiled=True),
        lax.all_gather(shards[8], "fsdp", axis=0, tiled=True),
        lax.all_gather(shards[9], "fsdp", axis=0, tiled=True),
        lax.all_gather(shards[10], "fsdp", axis=0, tiled=True),
        lax.all_gather(shards[11], "fsdp", axis=0, tiled=True),
        lax.all_gather(shards[12], "fsdp", axis=0, tiled=True),
    )
    (
        full_qkv,
        full_out,
        full_up,
        full_down,
        bias_qkv,
        pos_flat,
        bias_out,
        gain_first,
        shift_first,
        bias_up,
        bias_down,
        gain_second,
        shift_second,
    ) = gathered
    pos_all = pos_flat.reshape(2, PE, HD)

    def to_heads(flat_in):
        return flat_in.reshape(row_count, seq_len, HEADS, HD).transpose(0, 2, 1, 3)

    def from_heads(head_in):
        return head_in.transpose(0, 2, 1, 3).reshape(tok_count, model_width)

    flat_rows = tokens.reshape(tok_count, model_width)
    qkv_low = (
        jnp.dot(flat_rows, full_qkv, preferred_element_type=jnp.float32)
        + bias_qkv.astype(jnp.float32)
    ).astype(jnp.bfloat16)
    query_heads = to_heads(qkv_low[:, :model_width])
    key_heads = to_heads(qkv_low[:, model_width : 2 * model_width])
    value_heads = to_heads(qkv_low[:, 2 * model_width :])
    freq_count = PE // 16
    freq_vals = jnp.exp(
        jnp.arange(freq_count).astype(jnp.float32) * (-math.log(10000.0) / freq_count)
    )
    angles = jnp.moveaxis(box_coords, 0, -1).astype(jnp.float32)[..., None] * freq_vals
    sin_vals = jnp.sin(angles)
    cos_vals = jnp.cos(angles)
    feat_shape = (row_count, 1, seq_len, PE)
    box_feats = jnp.stack([sin_vals, cos_vals], axis=-1).reshape(feat_shape)
    sin_rep = jnp.stack([sin_vals, sin_vals], axis=-1).reshape(feat_shape)
    cos_sign = jnp.stack([-cos_vals, cos_vals], axis=-1).reshape(feat_shape)
    comb_query = jnp.concatenate([pos_all[1], pair_swap(pos_all[1])], axis=0)
    comb_key = jnp.concatenate([pos_all[0], pair_swap(pos_all[0])], axis=0)
    query_pos = jnp.einsum(
        "rhld,fd->rhlf", query_heads, comb_query, preferred_element_type=jnp.float32
    )
    key_pos = jnp.einsum("rhld,fd->rhlf", key_heads, comb_key, preferred_element_type=jnp.float32)
    turned_query = query_pos[..., PE:] * sin_rep + query_pos[..., :PE] * cos_sign
    turned_key = key_pos[..., PE:] * sin_rep + key_pos[..., :PE] * cos_sign
    feats_heads = jnp.broadcast_to(box_feats.astype(jnp.bfloat16), (row_count, HEADS, seq_len, PE))
    left_all = jnp.concatenate(
        [query_heads, turned_query.astype(jnp.bfloat16), feats_heads], axis=-1
    )
    right_all = jnp.concatenate([key_heads, feats_heads, turned_key.astype(jnp.bfloat16)], axis=-1)

    def row_forward(inputs):
        left_side, right_side, row_values, row_pages = inputs
        return attend_row(left_side, right_side, row_values, row_pages, score_scale)

    ctx_rows, total_rows = lax.map(row_forward, (left_all, right_all, value_heads, page_ids))
    ctx_low = from_heads(ctx_rows).astype(jnp.bfloat16)
    attn_out = jnp.dot(ctx_low, full_out, preferred_element_type=jnp.float32) + bias_out.astype(
        jnp.float32
    )
    first_sum = flat_rows.astype(jnp.float32) + attn_out
    hidden, norm_back_one = jax.vjp(
        layer_norm, first_sum, gain_first.astype(jnp.float32), shift_first.astype(jnp.float32)
    )
    hidden_low = hidden.astype(jnp.bfloat16)
    up_proj = jnp.dot(hidden_low, full_up, preferred_element_type=jnp.float32) + bias_up.astype(
        jnp.float32
    )
    activated, gelu_back = jax.vjp(gelu_exact, up_proj)
    act_low = activated.astype(jnp.bfloat16)
    ffn_out = jnp.dot(act_low, full_down, preferred_element_type=jnp.float32) + bias_down.astype(
        jnp.float32
    )
    result, norm_back_two = jax.vjp(
        layer_norm,
        hidden + ffn_out,
        gain_second.astype(jnp.float32),
        shift_second.astype(jnp.float32),
    )
    layer_out = result.reshape(row_count, seq_len, model_width).astype(jnp.bfloat16)
    again = (
        lax.all_gather(shards[0], "fsdp", axis=0, tiled=True),
        lax.all_gather(shards[1], "fsdp", axis=0, tiled=True),
        lax.all_gather(shards[2], "fsdp", axis=0, tiled=True),
        lax.all_gather(shards[3], "fsdp", axis=0, tiled=True),
        lax.all_gather(shards[4], "fsdp", axis=0, tiled=True),
        lax.all_gather(shards[5], "fsdp", axis=0, tiled=True),
        lax.all_gather(shards[6], "fsdp", axis=0, tiled=True),
        lax.all_gather(shards[7], "fsdp", axis=0, tiled=True),
        lax.all_gather(shards[8], "fsdp", axis=0, tiled=True),
        lax.all_gather(shards[9], "fsdp", axis=0, tiled=True),
        lax.all_gather(shards[10], "fsdp", axis=0, tiled=True),
        lax.all_gather(shards[11], "fsdp", axis=0, tiled=True),
        lax.all_gather(shards[12], "fsdp", axis=0, tiled=True),
    )
    back_qkv, back_out, back_up, back_down = (again[0], again[1], again[2], again[3])
    back_pos = again[5].reshape(2, PE, HD).astype(jnp.float32)
    back_comb_query = jnp.concatenate([back_pos[1], pair_swap(back_pos[1])], axis=0)
    back_comb_key = jnp.concatenate([back_pos[0], pair_swap(back_pos[0])], axis=0)
    grad_result = cotangent.reshape(tok_count, model_width).astype(jnp.float32)
    grad_second, grad_gain_two, grad_shift_two = norm_back_two(grad_result)
    grad_ffn = grad_second.astype(jnp.bfloat16)
    grad_w_down = jnp.einsum("nf,nd->fd", act_low, grad_ffn, preferred_element_type=jnp.float32)
    grad_b_down = jnp.sum(grad_ffn.astype(jnp.float32), axis=0)
    grad_act = jnp.einsum("nd,fd->nf", grad_ffn, back_down, preferred_element_type=jnp.float32)
    grad_up = gelu_back(grad_act)[0].astype(jnp.bfloat16)
    grad_w_up = jnp.einsum("nd,nf->df", hidden_low, grad_up, preferred_element_type=jnp.float32)
    grad_b_up = jnp.sum(grad_up.astype(jnp.float32), axis=0)
    grad_hidden = grad_second + jnp.einsum(
        "nf,df->nd", grad_up, back_up, preferred_element_type=jnp.float32
    )
    grad_first, grad_gain_one, grad_shift_one = norm_back_one(grad_hidden)
    grad_attn = grad_first.astype(jnp.bfloat16)
    grad_w_out = jnp.einsum("nc,nd->cd", ctx_low, grad_attn, preferred_element_type=jnp.float32)
    grad_b_out = jnp.sum(grad_attn.astype(jnp.float32), axis=0)
    grad_ctx = jnp.einsum(
        "nd,cd->nc", grad_attn, back_out, preferred_element_type=jnp.float32
    ).astype(jnp.bfloat16)

    def row_backward(inputs):
        left_side, right_side, row_values, row_pages, log_total, row_grad = inputs
        return attend_back(
            left_side, right_side, row_values, row_pages, log_total, row_grad, score_scale
        )

    grad_left, grad_right, grad_values = lax.map(
        row_backward, (left_all, right_all, value_heads, page_ids, total_rows, to_heads(grad_ctx))
    )
    grad_turn_query = grad_left[..., HD : HD + PE]
    grad_turn_key = grad_right[..., HD + PE :]
    grad_comb_q = jnp.concatenate([grad_turn_query * cos_sign, grad_turn_query * sin_rep], axis=-1)
    grad_comb_k = jnp.concatenate([grad_turn_key * cos_sign, grad_turn_key * sin_rep], axis=-1)
    grad_query = grad_left[..., :HD] + jnp.einsum(
        "rhlf,fd->rhld", grad_comb_q, back_comb_query, precision=lax.Precision.HIGHEST
    )
    grad_keys = grad_right[..., :HD] + jnp.einsum(
        "rhlf,fd->rhld", grad_comb_k, back_comb_key, precision=lax.Precision.HIGHEST
    )
    comb_from_query = jnp.einsum(
        "rhld,rhlf->fd",
        query_heads.astype(jnp.float32),
        grad_comb_q,
        precision=lax.Precision.HIGHEST,
    )
    comb_from_key = jnp.einsum(
        "rhld,rhlf->fd", key_heads.astype(jnp.float32), grad_comb_k, precision=lax.Precision.HIGHEST
    )
    grad_pos_key = comb_from_query[:PE] + pair_swap(comb_from_query[PE:])
    grad_pos_query = comb_from_key[:PE] + pair_swap(comb_from_key[PE:])
    grad_w_pos = jnp.stack([grad_pos_query, grad_pos_key]).reshape(2 * PE * HD)
    grad_qkv = jnp.concatenate(
        [from_heads(grad_query), from_heads(grad_keys), from_heads(grad_values)], axis=1
    ).astype(jnp.bfloat16)
    grad_w_qkv = jnp.einsum("nd,ne->de", flat_rows, grad_qkv, preferred_element_type=jnp.float32)
    grad_b_qkv = jnp.sum(grad_qkv.astype(jnp.float32), axis=0)
    grad_input = grad_first + jnp.einsum(
        "ne,de->nd", grad_qkv, back_qkv, preferred_element_type=jnp.float32
    )
    grad_tokens = grad_input.reshape(row_count, seq_len, model_width).astype(jnp.bfloat16)
    partials = (
        grad_w_qkv,
        grad_w_out,
        grad_w_up,
        grad_w_down,
        grad_b_qkv,
        grad_w_pos,
        grad_b_out,
        grad_gain_one,
        grad_shift_one,
        grad_b_up,
        grad_b_down,
        grad_gain_two,
        grad_shift_two,
    )
    shard_sums = (
        lax.psum_scatter(partials[0], "fsdp", scatter_dimension=0, tiled=True),
        lax.psum_scatter(partials[1], "fsdp", scatter_dimension=0, tiled=True),
        lax.psum_scatter(partials[2], "fsdp", scatter_dimension=0, tiled=True),
        lax.psum_scatter(partials[3], "fsdp", scatter_dimension=0, tiled=True),
        lax.psum_scatter(partials[4], "fsdp", scatter_dimension=0, tiled=True),
        lax.psum_scatter(partials[5], "fsdp", scatter_dimension=0, tiled=True),
        lax.psum_scatter(partials[6], "fsdp", scatter_dimension=0, tiled=True),
        lax.psum_scatter(partials[7], "fsdp", scatter_dimension=0, tiled=True),
        lax.psum_scatter(partials[8], "fsdp", scatter_dimension=0, tiled=True),
        lax.psum_scatter(partials[9], "fsdp", scatter_dimension=0, tiled=True),
        lax.psum_scatter(partials[10], "fsdp", scatter_dimension=0, tiled=True),
        lax.psum_scatter(partials[11], "fsdp", scatter_dimension=0, tiled=True),
        lax.psum_scatter(partials[12], "fsdp", scatter_dimension=0, tiled=True),
    )
    totals = (
        lax.psum(shard_sums[0].astype(jnp.bfloat16), "rep").astype(jnp.float32),
        lax.psum(shard_sums[1].astype(jnp.bfloat16), "rep").astype(jnp.float32),
        lax.psum(shard_sums[2].astype(jnp.bfloat16), "rep").astype(jnp.float32),
        lax.psum(shard_sums[3].astype(jnp.bfloat16), "rep").astype(jnp.float32),
        lax.psum(shard_sums[4].astype(jnp.bfloat16), "rep").astype(jnp.float32),
        lax.psum(shard_sums[5].astype(jnp.bfloat16), "rep").astype(jnp.float32),
        lax.psum(shard_sums[6].astype(jnp.bfloat16), "rep").astype(jnp.float32),
        lax.psum(shard_sums[7].astype(jnp.bfloat16), "rep").astype(jnp.float32),
        lax.psum(shard_sums[8].astype(jnp.bfloat16), "rep").astype(jnp.float32),
        lax.psum(shard_sums[9].astype(jnp.bfloat16), "rep").astype(jnp.float32),
        lax.psum(shard_sums[10].astype(jnp.bfloat16), "rep").astype(jnp.float32),
        lax.psum(shard_sums[11].astype(jnp.bfloat16), "rep").astype(jnp.float32),
        lax.psum(shard_sums[12].astype(jnp.bfloat16), "rep").astype(jnp.float32),
    )
    (
        sum_w_qkv,
        sum_w_out,
        sum_w_up,
        sum_w_down,
        sum_b_qkv,
        sum_w_pos,
        sum_b_out,
        sum_gain_one,
        sum_shift_one,
        sum_b_up,
        sum_b_down,
        sum_gain_two,
        sum_shift_two,
    ) = totals
    return (
        layer_out,
        grad_tokens,
        sum_w_qkv,
        sum_b_qkv,
        sum_w_pos,
        sum_w_out,
        sum_b_out,
        sum_gain_one,
        sum_shift_one,
        sum_w_up,
        sum_b_up,
        sum_w_down,
        sum_b_down,
        sum_gain_two,
        sum_shift_two,
    )


def solution(mesh):
    in_specs = (
        P(("fsdp", "rep"), None, None),
        P(("fsdp", "rep"), None),
        P(None, ("fsdp", "rep"), None),
        P("fsdp", None),
        P("fsdp"),
        P("fsdp"),
        P("fsdp", None),
        P("fsdp"),
        P("fsdp"),
        P("fsdp"),
        P("fsdp", None),
        P("fsdp"),
        P("fsdp", None),
        P("fsdp"),
        P("fsdp"),
        P("fsdp"),
        P(("fsdp", "rep"), None, None),
    )
    out_specs = (
        P(("fsdp", "rep"), None, None),
        P(("fsdp", "rep"), None, None),
        P("fsdp", None),
        P("fsdp"),
        P("fsdp"),
        P("fsdp", None),
        P("fsdp"),
        P("fsdp"),
        P("fsdp"),
        P("fsdp", None),
        P("fsdp"),
        P("fsdp", None),
        P("fsdp"),
        P("fsdp"),
        P("fsdp"),
    )
    return jax.shard_map(body, mesh=mesh, in_specs=in_specs, out_specs=out_specs, check_vma=False)
```

profile of v0, /device:TPU:0, one launch (start us, length us, event | category | flops | bytes accessed | tf_op | source)
XLA Modules:
  0.0 1125.1 jit_solution(646275522644799636)
XLA Ops:
  10.0 33.1 %all_gather.46 = bf16[24576]{0:T(1024)(128)(2,1)S(1)} all-gather(bf16[3072]{0:T(1024)(128)(2,1)} %param.26), channel_id=1, replica_groups=mesh['fsdp'=8,'rep'=4] {'fsdp'}, dimensions={0}, use_global_device_ids=true | all-gather | bytes 55296 | tf_op jit(solution)/shard_map/all_gather | solution.py:111
  53.1 38.1 %all-reduce.17 = (bf16[2304]{0:T(1024)(128)(2,1)S(1)}, bf16[768]{0:T(1024)(128)(2,1)S(1)}, bf16[768]{0:T(1024)(128)(2,1)S(1)}, bf16[768]{0:T(1024)(128)(2,1)S(1)...) all-reduce(bf16[2304]{0:T(1024)(128)(2,1)S(1)} %dynamic-update-slic, ...), channel_id=1, replica_groups=mesh['fsdp'=8,'rep'=4] {'fsdp'}, use_global_device_ids=true, to_apply=%add | all-reduce | flops 6912 | bytes 27648
  94.2 26.3 %all-gather = bf16[8,1,384]{2,1,0:T(2,128)(2,1)S(1)} all-gather(bf16[1,1,384]{2,1,0:T(2,128)(2,1)S(1)} %reshape.371), channel_id=1, replica_groups=mesh['fsdp'=8,'rep'=4] {'fsdp'}, dimensions={0}, use_global_device_ids=true | all-gather | bytes 6912 | tf_op jit(solution)/shard_map/all_gather | solution.py:115
  175.7 13.3 %fusion.98 = (bf16[2,12,512,192]{2,3,1,0:T(8,128)(2,1)}, bf16[2,12,512,192]{2,3,1,0:T(8,128)(2,1)}) fusion(f32[2,12,512,384]{2,3,1,0:T(8,128)} %fusion.134, f32[2,512,192]{1,2,0:T(8,128)} %copy.174, f32[2,512,192]{1,2,0:T(8,128)} %copy.172, f32[2,12,512,384]{2,3,1,0:T(8,128)S(1)} %fusion.131), kind=kLoop, calls=%fused_computation.103 | loop fusion | flops 18874368 | bytes 48758784 | tf_op jit(solution)/shard_map/convert_element_type | solution.py:174
  203.8 50.8 %while.26 = (s32[]{:T(128)}, bf16[2,12,512,64]{2,3,1,0:T(8,128)(2,1)}, f32[2,12,512,1]{2,1,3,0:T(8,128)}, s32[2,512]{1,0:T(2,128)S(1)}, bf16[2,12,512,448]{2,3,1...) while((s32[]{:T(128)}, ...), condition=%wide.region_3.4_spmd, body=%wide.region_0.3_spmd.sunk | while | flops 3256084480 | bytes 102719608 | solution.py:180
  204.2 12.8 %fusion.195 = (f32[12,512]{1,0:T(8,128)S(1)}, f32[12,512,512]{1,2,0:T(8,128)}) fusion(pred[512,512]{0,1:T(8,128)(4,1)S(1)} %broadcast_compare_fusion.4, bf16[2,12,512,448]{2,3,1,0:T(8,128)(2,1)} %get-tuple-element.507, s32[]{:T(128)S(6)} %copy.269, bf16[2,12,512,448]{2,3,1,0:T(8,128)(2,1)} %get-tuple-element.506), kind=kOutput, calls=%fused_computation.3.clone.1 | convolution fusion | flops 2828003328 | bytes 23880704 | tf_op jit(solution)/shard_map/while/body/eval_jaxpr/hie,hje->hij/dot_general | solution.py:32
  229.5 12.7 %fusion.195 = (f32[12,512]{1,0:T(8,128)S(1)}, f32[12,512,512]{1,2,0:T(8,128)}) fusion(pred[512,512]{0,1:T(8,128)(4,1)S(1)} %broadcast_compare_fusion.4, bf16[2,12,512,448]{2,3,1,0:T(8,128)(2,1)} %get-tuple-element.507, s32[]{:T(128)S(6)} %copy.269, bf16[2,12,512,448]{2,3,1,0:T(8,128)(2,1)} %get-tuple-element.506), kind=kOutput, calls=%fused_computation.3.clone.1 | convolution fusion | flops 2828003328 | bytes 23880704 | tf_op jit(solution)/shard_map/while/body/eval_jaxpr/hie,hje->hij/dot_general | solution.py:32
  264.4 36.4 %multiply_convert_fusion.1 = (bf16[1024,3072]{1,0:T(8,128)(2,1)}, f32[1024,3072]{1,0:T(8,128)}, f32[1024,3072]{1,0:T(8,128)}) fusion(f32[3072]{0:T(1024)S(1)} %bitcast.258, bf16[768,3072]{1,0:T(8,128)(2,1)} %all-gather.10.cloned.1.call-done, f32[1024,768]{1,0:T(8,128)S(1)} %get-tuple-element.363, f32[768]{0:T(1024)S(1)} %copy-done.37, ...), kind=kOutput, calls=%fused_computation.85 | convolution fusion | flops 5043388416 | bytes 39348224 | tf_op jit(solution)/shard_map/dot_general | solution.py:190
  317.2 19.0 %convert_reduce_fusion = (f32[3072]{0:T(1024)}, bf16[1024,3072]{1,0:T(8,128)(2,1)}) fusion(f32[1024,3072]{1,0:T(8,128)} %get-tuple-element.334, bf16[1024,768]{1,0:T(8,128)(2,1)} %get-tuple-element.326, bf16[3072,768]{1,0:T(8,128)(2,1)} %all-gather.12.cloned.1.call-done, f32[1024,3072]{1,0:T(8,128)} %get-tuple-element.364, f32[3072]{0:T(1024)S(1)} %bitcast.259), kind=kOutput, calls=%fused_computation.83 | convolution fusion | flops 4885312512 | bytes 37773312 | tf_op jit(solution)/shard_map/nd,fd->nf/dot_general | solution.py:229
  363.1 155.6 %while.27 = (s32[]{:T(128)}, f32[2,12,512,448]{2,3,1,0:T(8,128)}, f32[2,12,512,448]{2,3,1,0:T(8,128)}, bf16[2,12,512,64]{2,3,1,0:T(8,128)(2,1)}, s32[2,512]{1,0:...) while((s32[]{:T(128)}, f32[2,12,512,448]{2,3,1,0:T(8,128)}, ...), condition=%wide.region_14.15_spmd, body=%wide.region_12.14_spmd.sunk | while | flops 9343087616 | bytes 188181648 | solution.py:250
  389.7 27.8 %bitcast_dynamic-update-slice_fusion.13 = f32[2,12,512,448]{2,3,1,0:T(8,128)} fusion(f32[2,12,512,448]{2,3,1,0:T(8,128)} %get-tuple-element.523, s32[]{:T(128)S(6)} %copy.279, bf16[2,12,512,448]{2,3,1,0:T(8,128)(2,1)} %get-tuple-element.537, f32[12,512,512]{1,2,0:T(8,128)} %fusion.206, f32[12,512,512]{1,2,0:T(8,128)} %fusion.207, ...), kind=kOutput, calls=%fused_computation.27.clone.1 | convolution fusion | flops 2853181952 | bytes 67437568 | tf_op jit(solution)/shard_map/while/body/eval_jaxpr/hij,hie->hje/dot_general | solution.py:59
  417.5 23.7 %bitcast_dynamic-update-slice_fusion.12 = f32[2,12,512,448]{2,3,1,0:T(8,128)} fusion(f32[2,12,512,448]{2,3,1,0:T(8,128)} %get-tuple-element.522, s32[]{:T(128)S(6)} %copy.279, f32[12,512,512]{1,2,0:T(8,128)} %fusion.206, f32[12,512,512]{1,2,0:T(8,128)} %fusion.207, f32[12,512]{1,0:T(8,128)S(1)} %dynamic-slice_bitcast_fusion.2, ...), kind=kOutput, calls=%fused_computation.28.clone.1 | convolution fusion | flops 2853181952 | bytes 67437568 | tf_op jit(solution)/shard_map/while/body/eval_jaxpr/hij,hje->hie/dot_general | solution.py:56
  467.2 27.8 %bitcast_dynamic-update-slice_fusion.13 = f32[2,12,512,448]{2,3,1,0:T(8,128)} fusion(f32[2,12,512,448]{2,3,1,0:T(8,128)} %get-tuple-element.523, s32[]{:T(128)S(6)} %copy.279, bf16[2,12,512,448]{2,3,1,0:T(8,128)(2,1)} %get-tuple-element.537, f32[12,512,512]{1,2,0:T(8,128)} %fusion.206, f32[12,512,512]{1,2,0:T(8,128)} %fusion.207, ...), kind=kOutput, calls=%fused_computation.27.clone.1 | convolution fusion | flops 2853181952 | bytes 67437568 | tf_op jit(solution)/shard_map/while/body/eval_jaxpr/hij,hie->hje/dot_general | solution.py:59
  494.9 23.6 %bitcast_dynamic-update-slice_fusion.12 = f32[2,12,512,448]{2,3,1,0:T(8,128)} fusion(f32[2,12,512,448]{2,3,1,0:T(8,128)} %get-tuple-element.522, s32[]{:T(128)S(6)} %copy.279, f32[12,512,512]{1,2,0:T(8,128)} %fusion.206, f32[12,512,512]{1,2,0:T(8,128)} %fusion.207, f32[12,512]{1,0:T(8,128)S(1)} %dynamic-slice_bitcast_fusion.2, ...), kind=kOutput, calls=%fused_computation.28.clone.1 | convolution fusion | flops 2853181952 | bytes 67437568 | tf_op jit(solution)/shard_map/while/body/eval_jaxpr/hij,hje->hie/dot_general | solution.py:56
  522.3 18.4 %slice_multiply_fusion.7 = (f32[2,12,512,192]{2,3,1,0:T(8,128)}, f32[2,12,512,192]{2,3,1,0:T(8,128)}, f32[2,12,512,192]{2,3,1,0:T(8,128)S(1)}, f32[2,12,512,192]{2,3,1,0:T(8,128)}) fusion(f32[2,12,512,448]{2,3,1,0:T(8,128)} %get-tuple-element.109, f32[2,512,192]{1,2,0:T(8,128)S(1)} %copy-done.17, f32[2,512,192]{1,2,0:T(8,128)S(1)} %copy-done.16, ...), kind=kLoop, calls=%fused_computation.114 | loop fusion | flops 9437184 | bytes 58195968 | tf_op jit(solution)/shard_map/mul | solution.py:255
  540.7 19.8 %fusion.110 = bf16[2,512,12,64]{1,3,2,0:T(8,128)(2,1)S(1)} fusion(f32[2,12,512,448]{2,3,1,0:T(8,128)} %get-tuple-element.109, f32[192,64]{0,1:T(8,128)S(1)} %copy-done.27, f32[192,64]{0,1:T(8,128)S(1)} %copy-done.28, f32[2,12,512,192]{2,3,1,0:T(8,128)} %get-tuple-element.340, f32[2,12,512,192]{2,3,1,0:T(8,128)} %get-tuple-element.339), kind=kOutput, calls=%fused_computation.151 | convolution fusion | flops 3630194688 | bytes 23691264 | tf_op jit(solution)/shard_map/rhlf,fd->rhld/dot_general | solution.py:257
  562.6 15.7 %fusion.111 = bf16[2,512,12,64]{1,3,2,0:T(8,128)(2,1)} fusion(f32[2,12,512,448]{2,3,1,0:T(8,128)} %get-tuple-element.110, f32[192,64]{0,1:T(8,128)S(1)} %copy-done.25, f32[192,64]{0,1:T(8,128)S(1)} %copy-done.26, f32[2,12,512,192]{2,3,1,0:T(8,128)S(1)} %get-tuple-element.347, f32[2,12,512,192]{2,3,1,0:T(8,128)} %get-tuple-element.348), kind=kOutput, calls=%fused_computation.152 | convolution fusion | flops 3630194688 | bytes 23691264 | tf_op jit(solution)/shard_map/rhlf,fd->rhld/dot_general | solution.py:260
  626.4 13.3 %fusion.117 = f32[384,64]{0,1:T(8,128)S(1)} fusion(bf16[2,512,12,64]{1,0,3,2:T(2,128)(2,1)S(1)} %copy-done.10, f32[2,12,512,192]{2,3,1,0:T(8,128)} %get-tuple-element.340, f32[2,12,512,192]{2,3,1,0:T(8,128)} %get-tuple-element.339), kind=kOutput, calls=%fused_computation.154 | convolution fusion | flops 3628597248 | bytes 20545536 | tf_op jit(solution)/shard_map/rhld,rhlf->fd/dot_general | solution.py:263
  640.3 13.0 %fusion.112 = f32[384,64]{0,1:T(8,128)S(1)} fusion(bf16[2,512,12,64]{1,0,3,2:T(2,128)(2,1)S(1)} %copy-done.8, f32[2,12,512,192]{2,3,1,0:T(8,128)} %copy-done.1, f32[2,12,512,192]{2,3,1,0:T(8,128)} %get-tuple-element.348), kind=kOutput, calls=%fused_computation.153 | convolution fusion | flops 3628597248 | bytes 20545536 | tf_op jit(solution)/shard_map/rhld,rhlf->fd/dot_general | solution.py:269
  657.4 35.1 %all-reduce.24 = (bf16[2304]{0:T(1024)(128)(2,1)S(1)}, bf16[24576]{0:T(1024)(128)(2,1)S(1)}, bf16[768]{0:T(1024)(128)(2,1)S(1)}, bf16[768]{0:T(1024)(128)(2,1)S(...) all-reduce(f32[2304]{0:T(1024)S(1)} %convert_reduce_fusion.1, ...), channel_id=3, replica_groups=mesh['fsdp'=8,'rep'=4] {'fsdp'}, use_global_device_ids=true, to_apply=%region_18.19.clone | all-reduce | flops 34560 | bytes 207360
  710.3 18.5 %reduce-scatter.13.cloned.1.call-done = f32[96,2304]{1,0:T(8,128)} async-done(((f32[768,2304]{1,0:T(8,128)}), f32[96,2304]{1,0:T(8,128)}) %reduce-scatter.13.cloned.1.call-update) | async-done | bytes 884752
  731.0 162.6 %reduce-scatter.9.cloned.1.call-done = f32[96,3072]{1,0:T(8,128)} async-done(((f32[768,3072]{1,0:T(8,128)}), f32[96,3072]{1,0:T(8,128)}) %reduce-scatter.9.cloned.1.call-update) | async-done | bytes 1179664 | tf_op jit(solution)/shard_map/reduce_scatter | solution.py:302
  895.8 162.7 %reduce-scatter.11.cloned.1.call-done = f32[384,768]{1,0:T(8,128)} async-done(((f32[3072,768]{1,0:T(8,128)}), f32[384,768]{1,0:T(8,128)}) %reduce-scatter.11.cloned.1.call-update) | async-done | bytes 1179664 | tf_op jit(solution)/shard_map/reduce_scatter | solution.py:303
  1069.3 40.8 %all-reduce.23.cloned.1.call-done = (bf16[96,2304]{0,1:T(8,128)(2,1)}, bf16[96,768]{1,0:T(8,128)(2,1)}, bf16[96,3072]{1,0:T(8,128)(2,1)}, bf16[384,768]{1,0:T(8,128)(2,1)}) async-done(((bf16[96,2304]{0,1:T(8,128)(2,1)}, bf16[96,768]{1,0:T(8,128)(2,1)}, bf16[96,3072]{1,0:T(8,128)(2,1)}, bf16[384,768]{1,0:T(8,128)(2,1)}), (bf16[96,2304]{0,1:T(8,128)(2,1)}, bf16[96,768]{1,0:T(8,128)(2,1)}, ...) | async-done | bytes 1769488 | tf_op jit(solution)/shard_map/psum | solution.py:315
  (313 shorter events, 310.5 us)
Async XLA Ops:
  7.2 126.7 %all-gather.6.cloned.1.call-start = ((), (), s32[]{:S(2)}) async-start(), calls=%async_computation.4 | async-start | bytes 3981312 | tf_op jit(solution)/shard_map/all_gather | solution.py:106
  7.9 252.0 %all-gather.8.cloned.1.call-start = ((), (), s32[]{:S(2)}) async-start(), calls=%async_computation.5 | async-start | bytes 1327104 | tf_op jit(solution)/shard_map/all_gather | solution.py:107
  8.7 255.6 %all-gather.10.cloned.1.call-start = ((), (), s32[]{:S(2)}) async-start(), calls=%async_computation.6 | async-start | bytes 5308416 | tf_op jit(solution)/shard_map/all_gather | solution.py:108
  9.4 291.4 %all-gather.12.cloned.1.call-start = ((), (), s32[]{:S(2)}) async-start(), calls=%async_computation.7 | async-start | bytes 5308416 | tf_op jit(solution)/shard_map/all_gather | solution.py:109
  10.0 698.7 %reduce-scatter.7.cloned.1.call-start = ((), (), s32[]{:S(2)}) async-start(), calls=%async_computation.8 | async-start | bytes 2654208 | tf_op jit(solution)/shard_map/reduce_scatter | solution.py:301
  153.8 10.9 copy-start.31
  153.8 10.9 copy-start.32
  191.4 12.5 %copy-start.35 = (s32[2,512]{1,0:T(2,128)S(1)}, s32[2,512]{1,0:T(2,128)}, u32[]{:S(2)}) copy-start(s32[2,512]{1,0:T(2,128)} %param.22) | copy-start | bytes 12292
  263.8 82.6 %copy-start.2 = (f32[1024,768]{1,0:T(8,128)}, f32[1024,768]{1,0:T(8,128)S(1)}, u32[]{:S(2)}) copy-start(f32[1024,768]{1,0:T(8,128)S(1)} %get-tuple-element.363) | copy-start | bytes 9437188
  263.8 82.6 %copy-start.21 = (f32[1024]{0:T(1024)}, f32[1024]{0:T(1024)S(1)}, u32[]{:S(2)}) copy-start(f32[1024]{0:T(1024)S(1)} %broadcast_multiply_fusion.1) | copy-start | bytes 12292
  264.3 82.1 %copy-start.23 = (f32[1024]{0:T(1024)}, f32[1024]{0:T(1024)S(1)}, u32[]{:S(2)}) copy-start(f32[1024]{0:T(1024)S(1)} %fusion.137) | copy-start | bytes 12292
  264.3 36.4 %copy-start.50 = (f32[768]{0:T(1024)S(1)}, f32[768]{0:T(1024)}, u32[]{:S(2)}) copy-start(f32[768]{0:T(1024)} %convert_element_type.230) | copy-start | bytes 9220
  300.8 10.0 copy-start.11
  300.8 10.0 copy-start.39
  361.7 367.1 %reduce-scatter.13.cloned.1.call-start = ((), (), s32[]{:S(2)}) async-start(), calls=%async_computation.11 | async-start | bytes 7962624
  522.3 18.4 %copy-start.27 = (f32[192,64]{0,1:T(8,128)S(1)}, f32[192,64]{0,1:T(8,128)}, u32[]{:S(2)}) copy-start(f32[192,64]{0,1:T(8,128)} %copy.188) | copy-start | bytes 147460
  522.3 18.4 %copy-start.28 = (f32[192,64]{0,1:T(8,128)S(1)}, f32[192,64]{0,1:T(8,128)}, u32[]{:S(2)}) copy-start(f32[192,64]{0,1:T(8,128)} %copy.187) | copy-start | bytes 147460
  540.7 21.9 %copy-start.1 = (f32[2,12,512,192]{2,3,1,0:T(8,128)}, f32[2,12,512,192]{2,3,1,0:T(8,128)S(1)}, u32[]{:S(2)}) copy-start(f32[2,12,512,192]{2,3,1,0:T(8,128)S(1)} %get-tuple-element.347) | copy-start | bytes 28311556
  598.3 295.4 %reduce-scatter.9.cloned.1.call-start = ((), (), s32[]{:S(2)}) async-start(), calls=%async_computation.9 | async-start | bytes 10616832 | tf_op jit(solution)/shard_map/reduce_scatter | solution.py:302
  611.4 447.1 %reduce-scatter.11.cloned.1.call-start = ((), (), s32[]{:S(2)}) async-start(), calls=%async_computation.10 | async-start | bytes 10616832 | tf_op jit(solution)/shard_map/reduce_scatter | solution.py:303
  623.2 486.9 %all-reduce.23.cloned.1.call-start = ((), (), s32[]{:S(2)}) async-start(), calls=%async_computation.12 | async-start | bytes 3833856 | tf_op jit(solution)/shard_map/psum | solution.py:315
  626.4 13.8 %copy-start.8 = (bf16[2,512,12,64]{1,0,3,2:T(2,128)(2,1)S(1)}, bf16[2,512,12,64]{1,0,3,2:T(2,128)(2,1)}, u32[]{:S(2)}) copy-start(bf16[2,512,12,64]{1,0,3,2:T(2,128)(2,1)} %reshape.335) | copy-start | bytes 4718596
  654.0 406.7 %copy-start.14 = (f32[1024,768]{1,0:T(8,128)S(1)}, f32[1024,768]{1,0:T(8,128)}, u32[]{:S(2)}) copy-start(f32[1024,768]{1,0:T(8,128)} %copy-done.13) | copy-start | bytes 9437188
  654.0 406.7 %copy-start.43 = (f32[1024]{0:T(1024)S(1)}, f32[1024]{0:T(1024)}, u32[]{:S(2)}) copy-start(f32[1024]{0:T(1024)} %copy-done.42) | copy-start | bytes 12292
  (40 other events, 151.6 us)
Sparse Core Ops, SparseCore 0:
  10.2 68.5 all-gather.5
  81.0 39.8 all-gather.7
  123.0 78.0 all-gather.9
  203.1 77.6 all-gather.11
  361.9 66.4 reduce-scatter.6
  598.4 130.3 reduce-scatter.12
  732.4 161.2 reduce-scatter.8
  897.3 161.2 reduce-scatter.10
  1062.3 47.7 all-reduce.22
where the time goes:
time: 1130 us
  matrix products  388 us (34%)
  waiting for transfers between devices  387 us (34%)
  blocking collectives  143 us (13%)
  other arithmetic  95.8 us (8%)
  local copies, waits for them, and re-layouts  90.4 us (8%)
  between operations  19.3 us (2%)
    reduce_scatter x1, waiting for transfers between devices, body(): lax.psum_scatter(partials[3], 'fsdp', scatter_dimension=0, tiled=True)  163 us
    reduce_scatter x1, waiting for transfers between devices, body(): lax.psum_scatter(partials[2], 'fsdp', scatter_dimension=0, tiled=True)  163 us
    unnamed x2, blocking collectives  73.2 us
    dot_general x2, matrix products, attend_back(): jnp.einsum('hij,hie->hje', grad_logits, left_side, preferred_element_type...  55.5 us
    dot_general x4, matrix products, row_scores(): jnp.einsum('hie,hje->hij', left_side, right_side, preferred_element_type=...  50.1 us
    dot_general x2, matrix products, attend_back(): jnp.einsum('hij,hje->hie', grad_logits, right_side, preferred_element_typ...  47.3 us
    psum x1, waiting for transfers between devices, body(): lax.psum(shard_sums[0].astype(jnp.bfloat16), 'rep').astype(jnp.float32)  40.8 us
    dot_general x1, matrix products, body(): jnp.dot(hidden_low, full_up, preferred_element_type=jnp.float32)  36.4 us
  transfers between devices with their start and end apart: 9, of which 4 were waited for; matrix products, arithmetic and copies ran while one was open for 44% of the time, Pallas kernels for 0%

commit v1 on v0

v1 whole, which is shorter than its diff:
```python
import math

import jax
import jax.numpy as jnp
from jax import lax
from jax.experimental import pallas as pl
from jax.experimental.pallas import tpu as pltpu
from jax.sharding import PartitionSpec as P

HEADS = 12
HD = 64
PE = 192
LANES = 128
SCALE = 1.0 / math.sqrt(HD + 2 * PE)


norm_eps = 1e-12


def comb_weights(pos):
    pairs = pos.reshape(PE // 2, 2, HD)
    eye = jnp.eye(HD, dtype=pos.dtype)
    one = jnp.concatenate(
        [pairs[:, 0].T, eye[:, : HD // 2], pairs[:, 1].T, eye[:, HD // 2 :]], axis=1
    )
    none = jnp.zeros_like(one)
    return jnp.stack(
        [jnp.concatenate([one, none], axis=0), jnp.concatenate([none, one], axis=0)]
    )


def features(box_coords):
    coords = jnp.moveaxis(box_coords, 0, -1).reshape(-1, 8).astype(jnp.float32)
    freq_count = PE // 16
    freq_vals = jnp.exp(
        jnp.arange(freq_count).astype(jnp.float32) * (-math.log(10000.0) / freq_count)
    )
    angles = (coords[:, :, None] * freq_vals).reshape(coords.shape[0], PE // 2)
    spare = ((0, 0), (0, LANES - PE // 2))
    sines, cosines = jnp.sin(angles), jnp.cos(angles)
    return (
        jnp.pad(sines, spare),
        jnp.pad(-cosines, spare, constant_values=1.0),
        jnp.pad(cosines, spare, constant_values=1.0),
    )


def mm(a, b):
    return lax.dot_general(a, b, (((1,), (0,)), ((), ())), preferred_element_type=jnp.float32)


def mm_nt(a, b):
    return lax.dot_general(a, b, (((1,), (1,)), ((), ())), preferred_element_type=jnp.float32)


def mm_tn(a, b):
    return lax.dot_general(a, b, (((0,), (0,)), ((), ())), preferred_element_type=jnp.float32)


def spare_lanes(shape):
    return lax.broadcasted_iota(jnp.int32, shape, 1) >= PE // 2


def attend_kernel(
    x_ref, wq_ref, wk_ref, wv_ref, bq_ref, bk_ref, bv_ref, cq_ref, ck_ref,
    sn_ref, cn_ref, cp_ref, pc_ref, pr_ref,
    q_out, k_out, v_out, ctx_out, p_out, bias_ref,
):
    pair, row = pl.program_id(0), pl.program_id(1)

    @pl.when(pair == 0)
    def _():
        for b in range(2):
            same = pc_ref[pl.ds(256 * b, 256), :] == pr_ref[0, :, pl.ds(128 * b, 384)]
            bias_ref[row, b] = jnp.where(same, 0.0, -1e30)

    weights = jnp.concatenate([wq_ref[...], wk_ref[...], wv_ref[...]], axis=1)
    biases = jnp.concatenate([bq_ref[...], bk_ref[...], bv_ref[...]], axis=1)
    qkv = (mm(x_ref[...], weights) + biases.astype(jnp.float32)).astype(jnp.bfloat16)
    q, k, v = qkv[:, :LANES], qkv[:, LANES : 2 * LANES], qkv[:, 2 * LANES :]
    q_out[...] = q
    k_out[...] = k
    v_out[...] = v
    sn, cn, cp = sn_ref[...], cn_ref[...], cp_ref[...]
    spare = spare_lanes(sn.shape)
    sin_low = sn.astype(jnp.bfloat16)
    cos_low = jnp.where(spare, 0.0, cp).astype(jnp.bfloat16)
    parts = []
    for e in range(2):
        oq, ok = mm(q, cq_ref[e]), mm(k, ck_ref[e])
        q0, q1 = oq[:, :LANES], oq[:, LANES:]
        k0, k1 = ok[:, :LANES], ok[:, LANES:]
        lq0 = (q0 * cn + q1 * sn).astype(jnp.bfloat16)
        lq1 = (q0 * sn + q1 * cp).astype(jnp.bfloat16)
        lk0 = (k0 * cn + k1 * sn).astype(jnp.bfloat16)
        lk1 = (k0 * sn + k1 * cp).astype(jnp.bfloat16)
        m0 = jnp.where(spare, lk0, sin_low)
        m1 = jnp.where(spare, lk1, cos_low)
        left = jnp.concatenate([lq0, lq1, sin_low, cos_low], axis=1)
        right = jnp.concatenate([m0, m1, lk0, lk1], axis=1)
        halves = []
        for b in range(2):
            s = mm_nt(left[256 * b : 256 * b + 256], right[128 * b : 128 * b + 384])
            s = s * SCALE + bias_ref[row, b]
            s = jnp.exp(s - jnp.max(s, axis=1, keepdims=True))
            p = (s * (1.0 / jnp.sum(s, axis=1, keepdims=True))).astype(jnp.bfloat16)
            p_out[0, e, b] = p
            halves.append(mm(p, v[128 * b : 128 * b + 384]))
        parts.append(jnp.concatenate(halves, axis=0))
    first = lax.broadcasted_iota(jnp.int32, parts[0].shape, 1) < HD
    ctx_out[...] = jnp.where(first, parts[0], parts[1]).astype(jnp.bfloat16)


def attend(x, w_qkv, b_qkv, comb_q, comb_k, feats, page_ids):
    tokens, width = x.shape
    rows, length = page_ids.shape
    pairs = width // LANES
    row_block = lambda w: pl.BlockSpec((length, w), lambda p, r: (r, 0))
    pair_block = pl.BlockSpec((length, LANES), lambda p, r: (r, p))
    weight = lambda at: pl.BlockSpec((width, LANES), lambda p, r: (0, at * pairs + p))
    bias = lambda at: pl.BlockSpec((1, LANES), lambda p, r: (0, at * pairs + p))
    whole = lambda s: pl.BlockSpec(s, lambda p, r: (0,) * len(s))
    slab = jax.ShapeDtypeStruct((tokens, width), jnp.bfloat16)
    b2 = b_qkv.reshape(1, -1)
    return pl.pallas_call(
        attend_kernel,
        name="attend",
        grid=(pairs, rows),
        in_specs=[
            row_block(width), weight(0), weight(1), weight(2), bias(0), bias(1), bias(2),
            whole(comb_q.shape), whole(comb_k.shape),
            row_block(LANES), row_block(LANES), row_block(LANES),
            row_block(1), pl.BlockSpec((1, 1, length), lambda p, r: (r, 0, 0)),
        ],
        out_specs=[
            pair_block, pair_block, pair_block, pair_block,
            pl.BlockSpec((1, 2, 2, 256, 384), lambda p, r: (r, p, 0, 0, 0)),
        ],
        out_shape=[slab, slab, slab, slab,
                   jax.ShapeDtypeStruct((rows, 2 * pairs, 2, 256, 384), jnp.bfloat16)],
        scratch_shapes=[pltpu.VMEM((rows, 2, 256, 384), jnp.float32)],
        compiler_params=pltpu.CompilerParams(vmem_limit_bytes=48 << 20),
    )(x, w_qkv, w_qkv, w_qkv, b2, b2, b2, comb_q, comb_k, *feats,
      page_ids.reshape(tokens, 1), page_ids.reshape(rows, 1, length))


def attend_back_kernel(
    q_ref, k_ref, v_ref, p_ref, dctx_ref, cq_ref, ck_ref, sn_ref, cn_ref, cp_ref,
    dq_out, dk_out, dv_out, gp_out,
):
    @pl.when((pl.program_id(0) == 0) & (pl.program_id(1) == 0))
    def _():
        gp_out[...] = jnp.zeros_like(gp_out)

    q, k, v, dctx = q_ref[...], k_ref[...], v_ref[...], dctx_ref[...]
    sn, cn, cp = sn_ref[...], cn_ref[...], cp_ref[...]
    spare = spare_lanes(sn.shape)
    sin_low = sn.astype(jnp.bfloat16)
    cos_low = jnp.where(spare, 0.0, cp).astype(jnp.bfloat16)
    first = lax.broadcasted_iota(jnp.int32, q.shape, 1) < HD
    dq = dk = None
    dvs = []
    for e in range(2):
        mine = first if e == 0 else ~first
        oq, ok = mm(q, cq_ref[e]).astype(jnp.bfloat16), mm(k, ck_ref[e]).astype(jnp.bfloat16)
        mix_q = jnp.concatenate(
            [jnp.where(spare, oq[:, :LANES], sin_low), jnp.where(spare, oq[:, LANES:], cos_low)], axis=1
        )
        mix_k = jnp.concatenate(
            [jnp.where(spare, ok[:, :LANES], sin_low), jnp.where(spare, ok[:, LANES:], cos_low)], axis=1
        )
        dc = jnp.where(mine, dctx, jnp.zeros_like(dctx))
        dleft, dright, dval = [], [], []
        for b in range(2):
            qs, ks = slice(256 * b, 256 * b + 256), slice(128 * b, 128 * b + 384)
            p_low = p_ref[0, e, b]
            p = p_low.astype(jnp.float32)
            dp = mm_nt(dc[qs], v[ks])
            inner = jnp.sum(dp * p, axis=1, keepdims=True)
            dt = (p * (dp - inner) * SCALE).astype(jnp.bfloat16)
            dleft.append(mm(dt, mix_k[ks]))
            dright.append(mm_tn(dt, mix_q[qs]))
            dval.append(mm_tn(p_low, dctx[qs]))
        dl = jnp.concatenate(dleft, axis=0)

        def joined(pieces):
            a, c = pieces
            return jnp.concatenate([a[:128], a[128:] + c[:256], c[256:]], axis=0)

        dr = joined(dright)
        dvs.append(joined(dval))
        for side, grad in (("q", dl), ("k", dr)):
            g0, g1 = grad[:, :LANES], grad[:, LANES:]
            turned = jnp.concatenate([g0 * cn + g1 * sn, g0 * sn + g1 * cp], axis=1).astype(jnp.bfloat16)
            if side == "q":
                part = mm_nt(turned, cq_ref[e])
                dq = part if dq is None else dq + part
                gp_out[1, e] += mm_tn(q, turned)
            else:
                part = mm_nt(turned, ck_ref[e])
                dk = part if dk is None else dk + part
                gp_out[0, e] += mm_tn(k, turned)
    dq_out[...] = dq.astype(jnp.bfloat16)
    dk_out[...] = dk.astype(jnp.bfloat16)
    dv_out[...] = jnp.where(first, dvs[0], dvs[1]).astype(jnp.bfloat16)


def attend_back(q, k, v, probs, dctx, comb_q, comb_k, feats):
    tokens, width = q.shape
    rows = probs.shape[0]
    length = tokens // rows
    pairs = width // LANES
    row_block = lambda w: pl.BlockSpec((length, w), lambda p, r: (r, 0))
    pair_block = pl.BlockSpec((length, LANES), lambda p, r: (r, p))
    whole = lambda s: pl.BlockSpec(s, lambda p, r: (0,) * len(s))
    slab = jax.ShapeDtypeStruct((tokens, width), jnp.bfloat16)
    gp_shape = (2, 2, LANES, 2 * LANES)
    return pl.pallas_call(
        attend_back_kernel,
        name="attend_back",
        grid=(pairs, rows),
        in_specs=[
            pair_block, pair_block, pair_block,
            pl.BlockSpec((1, 2, 2, 256, 384), lambda p, r: (r, p, 0, 0, 0)), pair_block,
            whole(comb_q.shape), whole(comb_k.shape),
            row_block(LANES), row_block(LANES), row_block(LANES),
        ],
        out_specs=[pair_block, pair_block, pair_block, whole(gp_shape)],
        out_shape=[slab, slab, slab, jax.ShapeDtypeStruct(gp_shape, jnp.float32)],
        compiler_params=pltpu.CompilerParams(vmem_limit_bytes=48 << 20),
    )(q, k, v, probs, dctx, comb_q, comb_k, *feats)


def pos_grad(gp):
    own = gp[:, 0, :HD] + gp[:, 1, HD:]
    even, odd = own[:, :, : PE // 2], own[:, :, LANES : LANES + PE // 2]
    return jnp.stack([even, odd], axis=-1).reshape(2, HD, PE).transpose(0, 2, 1).reshape(-1)


TILE = 256
FF_BLOCK = 768
ROOT_HALF = math.sqrt(0.5)
ROOT_TWO_PI = 1.0 / math.sqrt(2.0 * math.pi)


def normed(values):
    offset = values - jnp.mean(values, axis=1, keepdims=True)
    inverse = lax.rsqrt(jnp.mean(offset * offset, axis=1, keepdims=True) + norm_eps)
    return offset * inverse, inverse


def normed_back(grad, normal, inverse):
    return inverse * (
        grad
        - jnp.mean(grad, axis=1, keepdims=True)
        - normal * jnp.mean(grad * normal, axis=1, keepdims=True)
    )


def middle_kernel(
    x_ref, ctx_ref, cot_ref, w_out_ref, w_up_ref, w_down_ref, vec_ref, b_up_ref,
    out_ref, act_ref, h_ref, dffn_ref, dup_ref, dattn_ref, dz1_ref, dctx_ref, sums_ref, sum_up_ref,
    slope_ref,
):
    @pl.when(pl.program_id(0) == 0)
    def _():
        sums_ref[...] = jnp.zeros_like(sums_ref)
        sum_up_ref[...] = jnp.zeros_like(sum_up_ref)

    f32, bf16 = jnp.float32, jnp.bfloat16
    vec = vec_ref[...].astype(f32)
    b_out, gain1, shift1, b_down, gain2, shift2 = (vec[i : i + 1] for i in range(6))
    z1 = x_ref[...].astype(f32) + mm(ctx_ref[...], w_out_ref[...]) + b_out
    n1, r1 = normed(z1)
    h = n1 * gain1 + shift1
    h_low = h.astype(bf16)
    h_ref[...] = h_low
    z2 = h + b_down
    hidden = w_up_ref.shape[1]
    for j in range(0, hidden, FF_BLOCK):
        at = slice(j, j + FF_BLOCK)
        up = mm(h_low, w_up_ref[:, at]) + b_up_ref[:, at].astype(f32)
        phi = 0.5 * (1.0 + lax.erf(up * ROOT_HALF))
        slope_ref[:, at] = phi + up * (ROOT_TWO_PI * jnp.exp(-0.5 * up * up))
        act = (up * phi).astype(bf16)
        act_ref[:, at] = act
        z2 = z2 + mm(act, w_down_ref[at, :])
    n2, r2 = normed(z2)
    out_ref[...] = (n2 * gain2 + shift2).astype(bf16)
    g = cot_ref[...].astype(f32)
    dz2 = normed_back(g * gain2, n2, r2)
    dffn = dz2.astype(bf16)
    dffn_ref[...] = dffn
    dh = dz2
    for j in range(0, hidden, FF_BLOCK):
        at = slice(j, j + FF_BLOCK)
        dup = (mm_nt(dffn, w_down_ref[at, :]) * slope_ref[:, at]).astype(bf16)
        dup_ref[:, at] = dup
        sum_up_ref[:, at] += jnp.sum(dup.astype(f32), axis=0, keepdims=True)
        dh = dh + mm_nt(dup, w_up_ref[:, at])
    dz1 = normed_back(dh * gain1, n1, r1)
    dattn = dz1.astype(bf16)
    dz1_ref[...] = dz1
    dattn_ref[...] = dattn
    dctx_ref[...] = mm_nt(dattn, w_out_ref[...]).astype(bf16)
    for i, v in enumerate((dattn.astype(f32), dh * n1, dh, dffn.astype(f32), g * n2, g)):
        sums_ref[i : i + 1, :] += jnp.sum(v, axis=0, keepdims=True)


def middle(x, ctx, cot, w_out, w_up, w_down, vecs, b_up):
    tokens, width = x.shape
    hidden = w_up.shape[1]
    tile = lambda w: pl.BlockSpec((TILE, w), lambda i: (i, 0))
    whole = lambda s: pl.BlockSpec(s, lambda i: (0,) * len(s), pipeline_mode=pl.Buffered(1))
    out = lambda w, t=jnp.bfloat16: jax.ShapeDtypeStruct((tokens, w), t)
    return pl.pallas_call(
        middle_kernel,
        name="middle",
        grid=(tokens // TILE,),
        in_specs=[
            tile(width), tile(width), tile(width), whole(w_out.shape), whole(w_up.shape),
            whole(w_down.shape), whole(vecs.shape), whole(b_up.shape),
        ],
        out_specs=[
            tile(width), tile(hidden), tile(width), tile(width), tile(hidden), tile(width),
            tile(width), tile(width),
            pl.BlockSpec((8, width), lambda i: (0, 0)), pl.BlockSpec((1, hidden), lambda i: (0, 0)),
        ],
        out_shape=[
            out(width), out(hidden), out(width), out(width), out(hidden), out(width),
            out(width, jnp.float32), out(width),
            jax.ShapeDtypeStruct((8, width), jnp.float32), jax.ShapeDtypeStruct((1, hidden), jnp.float32),
        ],
        scratch_shapes=[pltpu.VMEM((TILE, hidden), jnp.float32)],
        compiler_params=pltpu.CompilerParams(vmem_limit_bytes=58 << 20),
    )(x, ctx, cot, w_out, w_up, w_down, vecs, b_up)


def body(
    tokens, page_ids, box_coords, w_qkv, b_qkv, w_pos, w_out, b_out, gain_one, shift_one,
    w_up, b_up, w_down, b_down, gain_two, shift_two, cotangent,
):
    width = tokens.shape[-1]
    x = tokens.reshape(-1, width)
    devices = lax.axis_size("fsdp")
    small = (b_qkv, w_pos, b_up, b_out, gain_one, shift_one, b_down, gain_two, shift_two)
    sizes = [s.shape[0] for s in small]
    packed = lax.all_gather(jnp.concatenate(small), "fsdp", axis=0)
    pieces, at = [], 0
    for size in sizes:
        pieces.append(packed[:, at : at + size].reshape(-1))
        at += size
    f_b_qkv, f_pos, f_b_up = pieces[:3]
    vecs = jnp.pad(jnp.stack(pieces[3:]), ((0, 2), (0, 0)))
    f_qkv, f_out, f_up, f_down = (
        lax.all_gather(s, "fsdp", axis=0, tiled=True) for s in (w_qkv, w_out, w_up, w_down)
    )
    pos = f_pos.reshape(2, PE, HD)
    comb_q, comb_k = comb_weights(pos[1]), comb_weights(pos[0])
    feats = features(box_coords)
    q, k, v, ctx, probs = attend(x, f_qkv, f_b_qkv, comb_q, comb_k, feats, page_ids)
    cot = cotangent.reshape(-1, width)
    out, act, h_low, dffn, dup, dattn, dz1, dctx, sums, sum_up = middle(
        x, ctx, cot, f_out, f_up, f_down, vecs, f_b_up.reshape(1, -1)
    )

    def total(a, b):
        part = lax.dot_general(
            a, b, (((0,), (0,)), ((), ())), preferred_element_type=jnp.float32
        ).astype(jnp.bfloat16)
        mine = lax.psum_scatter(part, "fsdp", scatter_dimension=0, tiled=True)
        return lax.psum(mine, "rep").astype(jnp.float32)

    g_down, g_up, g_out = total(act, dffn), total(h_low, dup), total(ctx, dattn)
    dq, dk, dv, gp = attend_back(q, k, v, probs, dctx, comb_q, comb_k, feats)
    dqkv = jnp.concatenate([dq, dk, dv], axis=1)
    g_qkv = total(x, dqkv)
    grad_x = dz1 + lax.dot_general(
        dqkv, f_qkv, (((1,), (1,)), ((), ())), preferred_element_type=jnp.float32
    )
    sum_qkv = jnp.sum(dqkv.astype(jnp.float32), axis=0)
    vectors = (sum_qkv, pos_grad(gp), sum_up[0]) + tuple(sums[i] for i in range(6))
    flat = jnp.concatenate([g.reshape(devices, -1) for g in vectors], axis=1)
    summed = lax.psum(lax.psum_scatter(flat, "fsdp", scatter_dimension=0, tiled=True), "rep")[0]
    outs, at = [], 0
    for size in sizes:
        outs.append(summed[at : at + size])
        at += size
    g_b_qkv, g_pos, g_b_up, g_b_out, g_gain1, g_shift1, g_b_down, g_gain2, g_shift2 = outs
    return (
        out.reshape(tokens.shape), grad_x.astype(jnp.bfloat16).reshape(tokens.shape),
        g_qkv, g_b_qkv, g_pos, g_out, g_b_out, g_gain1, g_shift1,
        g_up, g_b_up, g_down, g_b_down, g_gain2, g_shift2,
    )


def solution(mesh):
    in_specs = (
        P(("fsdp", "rep"), None, None),
        P(("fsdp", "rep"), None),
        P(None, ("fsdp", "rep"), None),
        P("fsdp", None),
        P("fsdp"),
        P("fsdp"),
        P("fsdp", None),
        P("fsdp"),
        P("fsdp"),
        P("fsdp"),
        P("fsdp", None),
        P("fsdp"),
        P("fsdp", None),
        P("fsdp"),
        P("fsdp"),
        P("fsdp"),
        P(("fsdp", "rep"), None, None),
    )
    out_specs = (
        P(("fsdp", "rep"), None, None),
        P(("fsdp", "rep"), None, None),
        P("fsdp", None),
        P("fsdp"),
        P("fsdp"),
        P("fsdp", None),
        P("fsdp"),
        P("fsdp"),
        P("fsdp"),
        P("fsdp", None),
        P("fsdp"),
        P("fsdp", None),
        P("fsdp"),
        P("fsdp"),
        P("fsdp"),
    )
    return jax.shard_map(body, mesh=mesh, in_specs=in_specs, out_specs=out_specs, check_vma=False)
```

time: 1130 us -> 928 us (0.82)
  matrix products: 388 us -> 35.9 us
  waiting for transfers between devices: 387 us -> 685 us
  blocking collectives: 143 us -> 10.9 us
  Pallas kernels: 0 us -> 113 us
  other arithmetic: 95.8 us -> 14.3 us
  local copies, waits for them, and re-layouts: 90.4 us -> 52.1 us
    dot_general x32 -> x5, matrix products: 388 us -> 35.9 us  [the longest x4 28.1 us: total(): lax.dot_general(a, b, (((0,), (0,)), ((), ())), preferred_element_type=jn...]
    all_gather x4, waiting for transfers between devices: 0.03 us -> 222 us  [body(): lax.all_gather(s, 'fsdp', axis=0, tiled=True)]
    unnamed x10 -> x14, waiting for transfers between devices: 21.2 us -> 163 us
    pallas_call x0 -> x3, Pallas kernels: none -> 113 us  [the longest x1 39.9 us: attend(): pl.pallas_call(attend_kernel, name='attend', grid=(pairs, rows), in_specs...]
    unnamed x2 -> x0, blocking collectives: 73.2 us -> none
    reduce_scatter x3, waiting for transfers between devices: 325 us -> 264 us  [total(): mine = lax.psum_scatter(part, 'fsdp', scatter_dimension=0, tiled=True)]
    all_gather x2 -> x0, blocking collectives: 59.4 us -> none  [the longest x1 33.1 us: body(): lax.all_gather(shards[5], 'fsdp', axis=0, tiled=True)]
    convert_element_type x25 -> x4, other arithmetic: 34.4 us -> 5.14 us  [the longest x3 5.13 us: total(): return lax.psum(mine, 'rep').astype(jnp.float32)]
  transfers between devices with their start and end apart: 9 -> 11, of which waited for: 4 -> 10; matrix products, arithmetic and copies ran while one was open for 44% -> 7% of each run, Pallas kernels for 0% -> 4%
where the time goes in v1:
time: 928 us; the launch traced here: 927 us
  waiting for transfers between devices  685 us (74%)
  Pallas kernels  113 us (12%)
  local copies, waits for them, and re-layouts  52.1 us (6%)
  matrix products  35.9 us (4%)
  between operations  14.9 us (2%)
  other arithmetic  14.3 us (2%)
  blocking collectives  10.9 us (1%)
    reduce_scatter x3, waiting for transfers between devices, total(): mine = lax.psum_scatter(part, 'fsdp', scatter_dimension=0, tiled=True)  264 us
    all_gather x4, waiting for transfers between devices, body(): lax.all_gather(s, 'fsdp', axis=0, tiled=True)  222 us
    unnamed x14, waiting for transfers between devices  163 us
    pallas_call x1, Pallas kernels, attend(): pl.pallas_call(attend_kernel, name='attend', grid=(pairs, rows), in_specs...  39.9 us
    pallas_call x1, Pallas kernels, middle(): pl.pallas_call(middle_kernel, name='middle', grid=(tokens // TILE,), in_s...  36.9 us
    pallas_call x1, Pallas kernels, attend_back(): pl.pallas_call(attend_back_kernel, name='attend_back', grid=(pairs, rows)...  36.6 us
    psum x1, waiting for transfers between devices, total(): return lax.psum(mine, 'rep').astype(jnp.float32)  36 us
    dot_general x4, matrix products, total(): lax.dot_general(a, b, (((0,), (0,)), ((), ())), preferred_element_type=jn...  28.1 us
  transfers between devices with their start and end apart: 11, of which 10 were waited for; matrix products, arithmetic and copies ran while one was open for 7% of the time, Pallas kernels for 4%

profile of v1, /device:TPU:0, one launch (start us, length us, event | category | flops | bytes accessed | tf_op | source)
XLA Modules:
  0.0 926.8 jit_solution(9380012506104097238)
XLA Ops:
  9.2 6.2 concatenate.27
  22.7 65.7 %all-reduce.15.cloned.1.call-done = bf16[34560]{0:T(1024)(128)(2,1)} async-done(((bf16[34560]{0:T(1024)(128)(2,1)}), bf16[34560]{0:T(1024)(128)(2,1)}) %all-reduce.15.cloned.1.call-update) | async-done | bytes 69136
  92.6 62.6 %all-gather.6.cloned.1.call-done.wq_ref.wk_ref.wv_ref = bf16[768,2304]{1,0:T(8,128)(2,1)} async-done(((bf16[96,2304]{1,0:T(8,128)(2,1)}), bf16[768,2304]{1,0:T(8,128)(2,1)}) %all-gather.6.cloned.1.call-update) | async-done | bytes 3538960 | tf_op jit(solution)/shard_map/all_gather | solution.py:356
  155.2 39.9 %attend.1 = (bf16[1024,768]{1,0:T(8,128)(2,1)S(1)}, bf16[1024,768]{1,0:T(8,128)(2,1)S(1)}, bf16[1024,768]{1,0:T(8,128)(2,1)}, bf16[1024,768]{1,0:T(8,128)(2,1)}, bf16[2,12,2,256,384]{4,3,2,1,0:T(8,128)(2,1)}) custom-call(bf16[1024,768]{1,0:T(8,128)(2,1)} %bitcast.78, bf16[768,2304]{1,0:T(8,128)(2,1)} %all-gather.6.cloned.1.call-done.wq_ref.wk_ref.wv_ref, ...), custom_call_target="tpu_custom_call" | custom-call | tf_op jit(solution)/shard_map/attend/pallas_call | solution.py:125
  197.4 79.9 %all-gather.10.cloned.1.call-done.w_up_ref = bf16[768,3072]{1,0:T(8,128)(2,1)} async-done(((bf16[96,3072]{1,0:T(8,128)(2,1)}), bf16[768,3072]{1,0:T(8,128)(2,1)}) %all-gather.10.cloned.1.call-update) | async-done | bytes 4718608 | tf_op jit(solution)/shard_map/all_gather | solution.py:356
  277.3 79.8 %all-gather.12.cloned.1.call-done.w_down_ref = bf16[3072,768]{1,0:T(8,128)(2,1)} async-done(((bf16[384,768]{1,0:T(8,128)(2,1)}), bf16[3072,768]{1,0:T(8,128)(2,1)}) %all-gather.12.cloned.1.call-update) | async-done | bytes 4718608 | tf_op jit(solution)/shard_map/all_gather | solution.py:356
  357.0 36.9 %middle.1 = (bf16[1024,768]{1,0:T(8,128)(2,1)}, bf16[1024,3072]{1,0:T(8,128)(2,1)}, bf16[1024,768]{1,0:T(8,128)(2,1)}, bf16[1024,768]{1,0:T(8,128)(2,1)}, bf16[1...) custom-call(bf16[1024,768]{1,0:T(8,128)(2,1)} %bitcast.79, ...), custom_call_target="tpu_custom_call" | custom-call | tf_op jit(solution)/shard_map/middle/pallas_call | solution.py:316
  394.0 36.6 %attend_back.1 = (bf16[1024,768]{1,0:T(8,128)(2,1)S(1)}, bf16[1024,768]{1,0:T(8,128)(2,1)S(1)}, bf16[1024,768]{1,0:T(8,128)(2,1)}, f32[2,2,128,256]{3,2,1,0:T(8,128)S(1)}) custom-call(bf16[1024,768]{1,0:T(8,128)(2,1)} %copy-done, bf16[1024,768]{1,0:T(8,128)(2,1)} %copy-done.1, bf16[1024,768]{1,0:T(8,128)(2,1)} %get-tuple-element.39.v_ref, ...), custom_call_target="tpu_custom_call" | custom-call | tf_op jit(solution)/shard_map/attend_back/pallas_call | solution.py:218
  434.2 5.4 fusion
  439.6 5.8 copy.50
  446.8 3.9 convolution_convert_fusion.3
  450.7 9.3 convolution_convert_fusion
  461.4 9.6 %convolution_convert_fusion.1 = bf16[768,3072]{1,0:T(8,128)(2,1)} fusion(bf16[1024,768]{1,0:T(8,128)(2,1)S(1)} %copy-done.11, bf16[1024,3072]{1,0:T(8,128)(2,1)} %get-tuple-element.50), kind=kOutput, calls=%fused_computation.2 | convolution fusion | flops 4834197504 | bytes 12582912 | tf_op jit(solution)/shard_map/dot_general | solution.py:368
  475.7 3.7 convert_reduce_fusion
  494.9 7.8 add_convert_fusion
  502.7 20.7 %reduce-scatter.13.cloned.1.call-done = bf16[96,2304]{1,0:T(8,128)(2,1)} async-done(((bf16[768,2304]{1,0:T(8,128)(2,1)}), bf16[96,2304]{1,0:T(8,128)(2,1)}) %reduce-scatter.13.cloned.1.call-update) | async-done | bytes 442384
  525.5 66.3 %reduce-scatter.7.cloned.1.call-done = bf16[96,768]{1,0:T(8,128)(2,1)} async-done(((bf16[768,768]{1,0:T(8,128)(2,1)}), bf16[96,768]{1,0:T(8,128)(2,1)}) %reduce-scatter.7.cloned.1.call-update) | async-done | bytes 147472 | tf_op jit(solution)/shard_map/reduce_scatter | solution.py:371
  591.7 98.4 %reduce-scatter.11.cloned.1.call-done = bf16[384,768]{1,0:T(8,128)(2,1)} async-done(((bf16[3072,768]{1,0:T(8,128)(2,1)}), bf16[384,768]{1,0:T(8,128)(2,1)}) %reduce-scatter.11.cloned.1.call-update) | async-done | bytes 589840 | tf_op jit(solution)/shard_map/reduce_scatter | solution.py:371
  690.1 99.0 %reduce-scatter.9.cloned.1.call-done = bf16[96,3072]{1,0:T(8,128)(2,1)} async-done(((bf16[768,3072]{1,0:T(8,128)(2,1)}), bf16[96,3072]{1,0:T(8,128)(2,1)}) %reduce-scatter.9.cloned.1.call-update) | async-done | bytes 589840 | tf_op jit(solution)/shard_map/reduce_scatter | solution.py:371
  789.1 73.8 %all-reduce.17.cloned.1.call-done = f32[8,4320]{1,0:T(8,128)} async-done(((f32[8,4320]{1,0:T(8,128)}), f32[8,4320]{1,0:T(8,128)}) %all-reduce.17.cloned.1.call-update) | async-done | bytes 138256
  864.5 10.9 %psum.36 = f32[1,4320]{1,0:T(1,128)S(1)} all-reduce(f32[1,4320]{1,0:T(1,128)S(1)} %constant_dynamic-slice_fusion), channel_id=1, replica_groups=mesh['fsdp'=8,'rep'=4] {'rep'}, use_global_device_ids=true, to_apply=%region_4.5 | all-reduce | flops 4320 | bytes 34560 | tf_op jit(solution)/shard_map/psum | solution.py:384
  877.9 36.0 %all-reduce.19.cloned.1.call-done = (bf16[96,2304]{0,1:T(8,128)(2,1)}, bf16[96,768]{1,0:T(8,128)(2,1)}, bf16[96,3072]{1,0:T(8,128)(2,1)}, bf16[384,768]{1,0:T(8,128)(2,1)}) async-done(((bf16[96,2304]{0,1:T(8,128)(2,1)}, bf16[96,768]{1,0:T(8,128)(2,1)}, bf16[96,3072]{1,0:T(8,128)(2,1)}, bf16[384,768]{1,0:T(8,128)(2,1)}), (bf16[96,2304]{0,1:T(8,128)(2,1)}, bf16[96,768]{1,0:T(8,128)(2,1)}, ...) | async-done | bytes 1769488 | tf_op jit(solution)/shard_map/psum | solution.py:372
  914.0 2.2 convert_element_type.80
  916.2 2.2 convert_element_type.82
  (122 shorter events, 49.6 us)
Async XLA Ops:
  7.2 81.3 %all-reduce.15.cloned.1.call-start = ((), (), s32[]{:S(2)}) async-start(), calls=%async_computation.11 | async-start | bytes 139264
  15.7 0.6 copy-start.8
  16.4 138.8 %all-gather.6.cloned.1.call-start = ((), (), s32[]{:S(2)}) async-start(), calls=%async_computation.4 | async-start | bytes 3981312 | tf_op jit(solution)/shard_map/all_gather | solution.py:356
  17.2 180.2 %all-gather.8.cloned.1.call-start = ((), (), s32[]{:S(2)}) async-start(), calls=%async_computation.5 | async-start | bytes 1327104 | tf_op jit(solution)/shard_map/all_gather | solution.py:356
  17.9 259.4 %all-gather.10.cloned.1.call-start = ((), (), s32[]{:S(2)}) async-start(), calls=%async_computation.6 | async-start | bytes 5308416 | tf_op jit(solution)/shard_map/all_gather | solution.py:356
  18.5 338.6 %all-gather.12.cloned.1.call-start = ((), (), s32[]{:S(2)}) async-start(), calls=%async_computation.7 | async-start | bytes 5308416 | tf_op jit(solution)/shard_map/all_gather | solution.py:356
  19.1 504.3 %reduce-scatter.13.cloned.1.call-start = ((), (), s32[]{:S(2)}) async-start(), calls=%async_computation.12 | async-start | bytes 3981312
  20.0 2.4 copy-start.10
  195.1 1.2 copy-start
  196.2 1.2 copy-start.1
  430.5 1.4 copy-start.6
  430.7 3.5 copy-start.4
  432.1 2.1 copy-start.3
  445.4 1.4 copy-start.5
  445.4 146.3 %reduce-scatter.7.cloned.1.call-start = ((), (), s32[]{:S(2)}) async-start(), calls=%async_computation.8 | async-start | bytes 1327104 | tf_op jit(solution)/shard_map/reduce_scatter | solution.py:371
  450.6 239.4 %reduce-scatter.11.cloned.1.call-start = ((), (), s32[]{:S(2)}) async-start(), calls=%async_computation.10 | async-start | bytes 5308416 | tf_op jit(solution)/shard_map/reduce_scatter | solution.py:371
  460.0 1.4 copy-start.11
  460.0 329.1 %reduce-scatter.9.cloned.1.call-start = ((), (), s32[]{:S(2)}) async-start(), calls=%async_computation.9 | async-start | bytes 5308416 | tf_op jit(solution)/shard_map/reduce_scatter | solution.py:371
  471.0 391.9 %all-reduce.17.cloned.1.call-start = ((), (), s32[]{:S(2)}) async-start(), calls=%async_computation.13 | async-start | bytes 278528
  471.3 23.6 %copy-start.2 = (bf16[768,2304]{1,0:T(8,128)(2,1)S(1)}, bf16[768,2304]{1,0:T(8,128)(2,1)}, u32[]{:S(2)}) copy-start(bf16[768,2304]{1,0:T(8,128)(2,1)} %all-gather.6.cloned.1.call-done.wq_ref.wk_ref.wv_ref) | copy-start | bytes 10616836
  494.8 419.1 %all-reduce.19.cloned.1.call-start = ((), (), s32[]{:S(2)}) async-start(), calls=%async_computation.14 | async-start | bytes 3833856 | tf_op jit(solution)/shard_map/psum | solution.py:372
  914.0 4.4 copy-start.7
  914.0 5.6 copy-start.9
Sparse Core Ops, SparseCore 0:
  16.5 71.8 all-reduce.14
  90.6 64.5 all-gather.5
  157.4 39.7 all-gather.7
  199.2 78.0 all-gather.9
  279.3 77.6 all-gather.11
  445.5 77.8 reduce-scatter.12
  527.4 64.3 reduce-scatter.6
  595.4 94.6 reduce-scatter.10
  693.7 95.2 reduce-scatter.8
  792.8 70.0 all-reduce.16
  866.1 47.8 all-reduce.18
